TPU v7x, 32 devices: a whole 2x2x4 slice. The times are simulated.
32 devices in a mesh: dp: 4 (over y, x), expert: 8 (over z, core).
Axes of the slice: x: 2, y: 2, z: 4, core: 2. Of those that a mesh axis runs over, the one named last changes fastest.
Arguments:
- tokens: bfloat16 [2, 32, 256, 1024], P(None, ('dp', 'expert')), may hold values from -6 to 6
- segment_ids: int32 [2, 32, 256], P(None, ('dp', 'expert')), may hold values from 0 to 15, never falling along the last dimension, each value on 1 to 128 neighbouring positions
- routes: int32 [2, 32, 256, 1], P(None, ('dp', 'expert')), may hold values from 0 to 7
- cotangent: bfloat16 [2, 32, 256, 1024], P(None, ('dp', 'expert')), may hold values from -6 to 6
- w_qkv: bfloat16 [1024, 3072], P(('dp', 'expert')), may hold values from -0.25 to 0.25
- w_attn_out: bfloat16 [1024, 1024], P(('dp', 'expert')), may hold values from -0.5 to 0.5
- w_router: bfloat16 [1024, 8], P(('dp', 'expert')), may hold values from -0.125 to 0.125
- gain_attn: bfloat16 [1024], P(('dp', 'expert')), may hold values from 0.099609375 to 1.8984375
- gain_moe: bfloat16 [1024], P(('dp', 'expert')), may hold values from 0.099609375 to 1.8984375
- w_expert_in: bfloat16 [8, 1024, 4096], P('expert', 'dp'), may hold values from -0.1875 to 0.1875
- w_expert_out: bfloat16 [8, 4096, 1024], P('expert', 'dp'), may hold values from -0.75 to 0.75
Outputs:
- output: bfloat16 [2, 32, 256, 1024], P(None, ('dp', 'expert'))
- grad_tokens: float32 [2, 32, 256, 1024], P(None, ('dp', 'expert'))
- grad_qkv: float32 [1024, 3072], P(('dp', 'expert'))
- grad_attn_out: float32 [1024, 1024], P(('dp', 'expert'))
- grad_router: float32 [1024, 8], P(('dp', 'expert'))
- grad_gain_attn: float32 [1024], P(('dp', 'expert'))
- grad_gain_moe: float32 [1024], P(('dp', 'expert'))
- grad_expert_in: float32 [8, 1024, 4096], P('expert', 'dp')
- grad_expert_out: float32 [8, 4096, 1024], P('expert', 'dp')
Inputs may be any that keep to these rules, and one draw needn't show every extreme that they name: `segment_ids`: in each sequence the numbers never fall; a document spans 1 to 128 positions, and in each sequence one spans exactly that many.
All inputs are finite; a program needn't handle non-finite values.
Results may differ from a plain program's by a relative error of at most 0.014.
The roundings to bfloat16 on the way count: a program that leaves them out, or rounds other values in their place, can miss the bound.
Values may be sent and summed in bfloat16 or wider, within the bound.
A program may use at most 256 MiB of HBM per device.

v0:
```python
import functools
import math

import jax
import jax.numpy as jnp
from jax import lax
from jax.experimental import pallas as pl
from jax.experimental.pallas import tpu as pltpu
from jax.sharding import PartitionSpec as P

HEADS = 16
epsilon = 1e-05
masked_value = -1e30
pieces = 8
f32 = jnp.float32
bf16 = jnp.bfloat16

MESH = pl.DeviceIdType.MESH
DMA = pltpu.SemaphoreType.DMA


def flip(index, mask):
    bit = 1
    while bit <= mask:
        if mask & bit:
            index = index + bit - 2 * bit * ((index // bit) % 2)
        bit *= 2
    return index


def place_of(chips):
    block = lax.axis_index("dp")
    owner = lax.axis_index("expert")
    peer_x = {"dp": flip(block, 1)}
    peer_y = {"dp": flip(block, 2)}
    peer_core = {"expert": flip(owner, 1)}
    peers_z = [{"expert": flip(owner, 2 * k)} for k in range(chips)]
    return block, owner // 2, owner % 2, peer_x, peer_y, peer_core, peers_z


def greet(peers):
    barrier = pltpu.get_barrier_semaphore()
    for peer in peers:
        pl.semaphore_signal(barrier, inc=1, device_id=peer, device_id_type=MESH)
    pl.semaphore_wait(barrier, len(peers))


def send(src, dst, send_sem, recv_sem, peer):
    copy = pltpu.make_async_remote_copy(
        src_ref=src, dst_ref=dst, send_sem=send_sem, recv_sem=recv_sem,
        device_id=peer, device_id_type=MESH,
    )
    copy.start()
    return copy


def normalize(values):
    row_mean = jnp.mean(values, axis=-1, keepdims=True)
    centered = values - row_mean
    inv_scale = lax.rsqrt(jnp.mean(centered * centered, axis=-1, keepdims=True) + epsilon)
    return (centered * inv_scale, inv_scale)


def norm_back(grad_normed, normed, inv_scale):
    return inv_scale * (
        grad_normed
        - jnp.mean(grad_normed, axis=-1, keepdims=True)
        - normed * jnp.mean(grad_normed * normed, axis=-1, keepdims=True)
    )


def dot(a, b):
    return jnp.dot(a, b, preferred_element_type=f32)


def dot_nt(a, b):
    return lax.dot_general(a, b, (((1,), (1,)), ((), ())), preferred_element_type=f32)


def dot_tn(a, b):
    return lax.dot_general(a, b, (((0,), (0,)), ((), ())), preferred_element_type=f32)


def lanes_of(shape):
    return lax.broadcasted_iota(jnp.int32, shape, 1)


def rows_of(shape):
    return lax.broadcasted_iota(jnp.int32, shape, 0)


def column(row):
    return jnp.transpose(jnp.broadcast_to(row.astype(f32), (128, row.shape[1])))[:, :1]


def one_hot_of(route):
    return jnp.where(lanes_of((route.shape[0], 128)).astype(f32) == route, 1.0, 0.0)


def choose_slots(route, spots, experts):
    seq_len = route.shape[0]
    capacity = (9 * seq_len + 8 * experts - 1) // (8 * experts)
    one_hot = one_hot_of(route)
    square = (seq_len, seq_len)
    before = jnp.where(lanes_of(square) < rows_of(square), 1.0, 0.0).astype(bf16)
    place = jnp.sum(dot(before, one_hot.astype(bf16)) * one_hot, axis=1, keepdims=True)
    slot = jnp.where(place < capacity, route * (spots // experts) + place, -1.0)
    return jnp.where(lanes_of((seq_len, spots)).astype(f32) == slot, 1.0, 0.0).astype(bf16)


def allowed_pairs(segment_row):
    square = (segment_row.shape[1],) * 2
    same = column(segment_row) == segment_row.astype(f32)
    return (lanes_of(square) <= rows_of(square)) & same


def begin_kernel(
    chips,
    experts,
    tokens,
    segments,
    routes,
    cotangent,
    shard_qkv,
    shard_out,
    shard_small,
    w_in,
    w_out,
    attn_in,
    qkv,
    lse,
    mixed,
    residual,
    hidden,
    probs,
    gains,
    kept_full,
    full_in,
    full_out,
    got_g,
    got_h,
    full,
    slots_g,
    slots_h,
    hold_in,
    hold_out,
    own_sem,
    sz,
    rz,
    sx,
    rx,
    sy,
    ry,
    sc,
    rc,
    sw,
    rw,
    lw,
    sd,
    rd,
    se,
    re,
    ld,
):
    block, chip, core, peer_x, peer_y, peer_core, peers_z = place_of(chips)
    owner = lax.axis_index("expert")
    micros, seq_len, model_width = tokens.shape
    rows = shard_qkv.shape[0]
    width = full.shape[1]
    cut = (width // 128 + 1) // 2 * 128
    halves = (pl.ds(0, cut), pl.ds(cut, width - cut))
    every = pl.ds(0, width)
    half = w_in.shape[1] // 2
    row_y, row_x = block // 2, block % 2

    def part(origin, step, columns):
        start = ((flip(block, origin) * chips + flip(chip, step)) * 2 + core) * rows
        return full.at[pl.ds(pl.multiple_of(start, rows), rows), columns]

    own_copies = []
    for i, (src, at) in enumerate(
        ((shard_qkv, 0), (shard_out, 3 * model_width), (shard_small, 4 * model_width))
    ):
        dst = part(0, 0, pl.ds(at, src.shape[1]))
        own_copies.append(pltpu.make_async_copy(src, dst, own_sem.at[i]))
        own_copies[-1].start()
    others = [{"expert": lax.rem(owner + k, experts)} for k in range(1, experts)]
    greet([peer_x, peer_y] + others)
    for copy in own_copies:
        copy.wait()

    mine = part(0, 0, every)
    along_z = [None] + [send(mine, mine, sz.at[k], rz.at[k], peers_z[k]) for k in range(1, chips)]
    along_x = [[None] * 3 for _ in range(chips)]
    along_y = [[None] * 3 for _ in range(chips)]
    across = [[None] * 4 for _ in range(chips)]

    def to_core(k, origin):
        piece = part(origin, k, every)
        across[k][origin] = send(
            piece, piece, sc.at[k, origin], rc.at[k, origin], peer_core
        )

    def pass_on(k):
        along_x[k][1].wait_recv()
        to_core(k, 1)
        along_y[k][1].wait_recv()
        to_core(k, 2)
        along_x[k][2].wait_recv()
        along_y[k][2].wait_recv()
        to_core(k, 3)

    def spread(k):
        for turn in range(2):
            for copies, s, r, peer, side in (
                (along_x, sx, rx, peer_x, turn),
                (along_y, sy, ry, peer_y, 1 - turn),
            ):
                piece = part(0, k, halves[side])
                copies[k][turn] = send(piece, piece, s.at[k, turn], r.at[k, turn], peer)
        to_core(k, 0)

    def turn_corner(k):
        along_x[k][0].wait_recv()
        piece = part(1, k, halves[0])
        along_y[k][2] = send(piece, piece, sy.at[k, 2], ry.at[k, 2], peer_y)
        along_y[k][0].wait_recv()
        piece = part(2, k, halves[1])
        along_x[k][2] = send(piece, piece, sx.at[k, 2], rx.at[k, 2], peer_x)

    piece_rows = w_out.shape[0] // pieces
    out_x = []

    def send_piece():
        j = len(out_x)
        at = pl.ds(j * piece_rows, piece_rows)
        out_x.append(
            send(w_out.at[at], full_out.at[row_x, at], sw.at[3 + j], rw.at[3 + j], peer_x)
        )

    spread(0)

    def put_slots(slots, m, values):
        packed = dot_tn(choose_slots(column(routes[m]), experts * slots.shape[2], experts), values)
        packed = packed.astype(bf16)
        for e in range(experts):
            size = slots.shape[2]
            slots[m, e] = packed[e * size : (e + 1) * size]

    for m in range(micros):
        put_slots(slots_g, m, cotangent[m])

    for k in range(chips):
        if k:
            along_z[k].wait_recv()
            spread(k)
            pass_on(k - 1)
        turn_corner(k)
        if k < pieces // 2:
            send_piece()

    local_in = pltpu.make_async_copy(w_in.at[:, pl.ds(row_y * half, half)], hold_in, lw.at[0])
    local_out = pltpu.make_async_copy(w_out, hold_out, lw.at[1])
    local_in.start()
    local_out.start()
    from_y = send(
        w_in.at[:, pl.ds((1 - row_y) * half, half)], full_in.at[block], sw.at[0], rw.at[0], peer_y
    )
    from_x = send(
        w_in.at[:, pl.ds(row_y * half, half)], full_in.at[block], sw.at[1], rw.at[1], peer_x
    )
    while len(out_x) < pieces:
        send_piece()

    def slot_copies(way, slots, got, m):
        def to_owner(k):
            peer = lax.rem(owner + k, experts)
            return pltpu.make_async_remote_copy(
                src_ref=slots.at[m, peer],
                dst_ref=got.at[m, 0, owner],
                send_sem=sd.at[way, m, k],
                recv_sem=rd.at[way, m, k],
                device_id={"expert": peer},
                device_id_type=MESH,
            )

        def to_y(k):
            origin = lax.rem(owner - k + experts, experts)
            return pltpu.make_async_remote_copy(
                src_ref=got.at[m, 0, origin],
                dst_ref=got.at[m, 1, origin],
                send_sem=se.at[way, m, k],
                recv_sem=re.at[way, m, k],
                device_id=peer_y,
                device_id_type=MESH,
            )

        own = pltpu.make_async_copy(slots.at[m, owner], got.at[m, 0, owner], ld.at[way, m])
        return to_owner, to_y, own

    def start_slots(way, slots, got, m):
        to_owner, to_y, own = slot_copies(way, slots, got, m)
        own.start()

        @pl.loop(1, experts)
        def _(k):
            to_owner(k).start()

    def relay_slots(way, slots, got, m):
        to_owner, to_y, own = slot_copies(way, slots, got, m)
        own.wait()
        to_y(0).start()

        @pl.loop(1, experts)
        def _(k):
            to_owner(k).wait_recv()
            to_y(k).start()

    def end_slots(way, slots, got, m):
        to_owner, to_y, own = slot_copies(way, slots, got, m)

        @pl.loop(1, experts)
        def _(k):
            to_owner(k).wait_send()

        @pl.loop(0, experts)
        def _(k):
            to_y(k).wait()

    for m in range(micros):
        start_slots(0, slots_g, got_g, m)
    pass_on(chips - 1)
    for k in range(chips):
        for origin in range(4):
            across[k][origin].wait_recv()
    keep = pltpu.make_async_copy(full, kept_full, own_sem.at[3])
    keep.start()
    small = jnp.transpose(full[:, pl.ds(4 * model_width, 128)].astype(f32))
    gains[...] = small[experts : experts + 2]
    local_in.wait()
    local_out.wait()
    store_in = pltpu.make_async_copy(hold_in, full_in.at[block], lw.at[0])
    store_out = pltpu.make_async_copy(hold_out, full_out.at[row_x], lw.at[1])
    store_in.start()
    store_out.start()

    scale = 1.0 / math.sqrt(model_width // HEADS)
    low_half = lanes_of((seq_len, 128)) < 64
    diagonal = None
    for m in range(micros):
        x = tokens[m].astype(f32)
        attn_in[m] = (normalize(x)[0] * gains[0:1, :]).astype(bf16)

        @pl.loop(0, 3 * model_width // 512)
        def _(j):
            at = pl.ds(pl.multiple_of(j * 512, 512), 512)
            qkv[m, :, at] = dot(attn_in[m], full[:, at]).astype(bf16)

        allowed = allowed_pairs(segments[m])
        lse[m] = jnp.zeros(lse.shape[1:], f32)

        @pl.loop(0, model_width // 128)
        def _(pair):
            at = pl.multiple_of(pair * 128, 128)
            query = qkv[m, :, pl.ds(at, 128)]
            key = qkv[m, :, pl.ds(model_width + at, 128)]
            value = qkv[m, :, pl.ds(2 * model_width + at, 128)]
            outs = []
            for side in range(2):
                here = low_half if side == 0 else jnp.logical_not(low_half)
                scores = dot_nt(jnp.where(here, query, 0.0).astype(bf16), key) * scale
                masked = jnp.where(allowed, scores, masked_value)
                top = jnp.max(masked, axis=1, keepdims=True)
                weight = jnp.exp(masked - top)
                norm = jnp.sum(weight, axis=1, keepdims=True)
                outs.append(dot((weight / norm).astype(bf16), value))
                head = lanes_of(lse.shape[1:]) == 2 * pair + side
                lse[m] = jnp.where(head, top + jnp.log(norm), lse[m])
            mixed[m, :, pl.ds(at, 128)] = jnp.where(low_half, outs[0], outs[1]).astype(bf16)

        y1 = x + dot(mixed[m], full[:, pl.ds(3 * model_width, model_width)])
        residual[m] = y1
        low = (normalize(y1)[0] * gains[1:2, :]).astype(bf16)
        hidden[m] = low
        put_slots(slots_h, m, low)
        start_slots(1, slots_h, got_h, m)
        logits = dot(low, full[:, pl.ds(4 * model_width, 128)])
        real = lanes_of(logits.shape) < experts
        logits = jnp.where(real, logits, masked_value)
        weight = jnp.where(real, jnp.exp(logits - jnp.max(logits, axis=1, keepdims=True)), 0.0)
        probs[m] = weight / jnp.sum(weight, axis=1, keepdims=True)
        if m == 0:
            from_y.wait_recv()
            piece = full_in.at[flip(block, 2)]
            diagonal = send(piece, piece, sw.at[2], rw.at[2], peer_x)
        relay_slots(0, slots_g, got_g, m)
        if m:
            relay_slots(1, slots_h, got_h, m - 1)
    relay_slots(1, slots_h, got_h, micros - 1)

    for m in range(micros):
        end_slots(0, slots_g, got_g, m)
        end_slots(1, slots_h, got_h, m)
    keep.wait()
    store_in.wait()
    store_out.wait()
    from_y.wait_send()
    for copy in (from_x, diagonal, *out_x):
        copy.wait()
    for k in range(chips):
        if k:
            along_z[k].wait_send()
        for turn in range(3):
            along_x[k][turn].wait_send()
            along_y[k][turn].wait_send()
        for origin in range(4):
            across[k][origin].wait_send()


def begin_layer(tokens, segments, routes, cotangent, shards, w_in, w_out, chips):
    experts = 2 * chips
    micros, seq_len, model_width = tokens.shape
    capacity = (9 * seq_len + 8 * experts - 1) // (8 * experts)
    padded = (capacity + 7) // 8 * 8
    width = 4 * model_width + 128
    rows, half = w_in.shape[0], w_in.shape[1] // 2
    shape = jax.ShapeDtypeStruct
    vmem, hbm = pl.BlockSpec(memory_space=pltpu.VMEM), pl.BlockSpec(memory_space=pl.ANY)
    spots = (micros, experts, padded, model_width)
    return pl.pallas_call(
        functools.partial(begin_kernel, chips, experts),
        out_shape=[
            shape((micros, seq_len, model_width), bf16),
            shape((micros, seq_len, 3 * model_width), bf16),
            shape((micros, seq_len, 128), f32),
            shape((micros, seq_len, model_width), bf16),
            shape((micros, seq_len, model_width), f32),
            shape((micros, seq_len, model_width), bf16),
            shape((micros, seq_len, 128), f32),
            shape((2, model_width), f32),
            shape((model_width, width), bf16),
            shape((4, rows, half), bf16),
            shape((2,) + w_out.shape, bf16),
            shape((micros, 2, experts, padded, model_width), bf16),
            shape((micros, 2, experts, padded, model_width), bf16),
        ],
        in_specs=[vmem] * 4 + [hbm] * 5,
        out_specs=[vmem] * 8 + [hbm] * 5,
        scratch_shapes=[
            pltpu.VMEM((model_width, width), bf16),
            pltpu.VMEM(spots, bf16),
            pltpu.VMEM(spots, bf16),
            pltpu.VMEM((rows, half), bf16),
            pltpu.VMEM(w_out.shape, bf16),
            DMA((4,)),
            DMA((chips,)),
            DMA((chips,)),
            DMA((chips, 3)),
            DMA((chips, 3)),
            DMA((chips, 3)),
            DMA((chips, 3)),
            DMA((chips, 4)),
            DMA((chips, 4)),
            DMA((3 + pieces,)),
            DMA((3 + pieces,)),
            DMA((2,)),
            DMA((2, micros, experts)),
            DMA((2, micros, experts)),
            DMA((2, micros, experts)),
            DMA((2, micros, experts)),
            DMA((2, micros)),
        ],
        compiler_params=pltpu.CompilerParams(
            collective_id=1, has_side_effects=True, vmem_limit_bytes=60 * 2**20
        ),
        name="begin_layer",
    )(tokens, segments, routes, cotangent, *shards, w_in, w_out)


def expert_kernel(
    chips,
    experts,
    got_h,
    got_g,
    w_in_hbm,
    w_out_hbm,
    full,
    returned,
    grad_back,
    keep_in,
    send_in,
    grad_out,
    x_buf,
    gz_buf,
    w_in,
    w_out,
    router,
    act,
    gu,
    own,
    part,
    part_got,
    out_part,
    out_got,
    out_stage,
    in_part,
    in_stage,
    load,
    sy,
    ry,
    sz,
    rz,
    lz,
    sx,
    rx,
    st,
):
    block, chip, core, peer_x, peer_y, peer_core, peers_z = place_of(chips)
    owner = lax.axis_index("expert")
    micros, rows, model_width = got_h.shape
    half = w_in.shape[1]
    mine = rows // 2
    padded = part.shape[3]
    row_x = block % 2
    step = 256
    backs = (returned, grad_back)

    sources = [
        (got_h.at[0], x_buf.at[pl.ds(0, rows)]),
        (full.at[:, pl.ds(4 * model_width, 128)], router),
        (got_g.at[0], gz_buf.at[pl.ds(0, rows)]),
        (w_in_hbm, w_in),
        (w_out_hbm, w_out),
        (got_h.at[1], x_buf.at[pl.ds(rows, rows)]),
        (got_g.at[1], gz_buf.at[pl.ds(rows, rows)]),
    ]
    loads = []
    for i, (src, dst) in enumerate(sources):
        loads.append(pltpu.make_async_copy(src, dst, load.at[i]))
        loads[-1].start()
    greet(
        [peer_x, peer_y]
        + [{"expert": lax.rem(owner + k, experts)} for k in range(1, experts)]
    )

    def of(m):
        return pl.ds(m * rows, rows)

    def open_rows(m):
        logits = dot(x_buf[of(m), :], router[...])
        lanes = lanes_of(logits.shape)
        logits = jnp.where(lanes < experts, logits, masked_value)
        weight = jnp.exp(logits - jnp.max(logits, axis=1, keepdims=True))
        weight = jnp.where(lanes < experts, weight, 0.0)
        picked = jnp.sum(jnp.where(lanes == owner, weight, 0.0), axis=1, keepdims=True)
        gate = picked / jnp.sum(weight, axis=1, keepdims=True)
        gz_buf[of(m), :] = (gate * gz_buf[of(m), :].astype(f32)).astype(bf16)

        @pl.loop(0, half // step)
        def _(j):
            at = pl.ds(pl.multiple_of(j * step, step), step)
            u = dot(x_buf[of(m), :], w_in[:, at])
            back = dot_nt(gz_buf[of(m), :], w_out[at, :])
            root = math.sqrt(2.0 / math.pi)
            square = u * u
            bend = jnp.tanh(root * (u + 0.044715 * (u * square)))
            act[of(m), at] = (0.5 * u * (1.0 + bend)).astype(bf16)
            slope = 0.5 * (1.0 + bend) + 0.5 * u * (1.0 - bend * bend) * (
                root * (1.0 + (3.0 * 0.044715) * square)
            )
            gu[of(m), at] = (back * slope).astype(bf16)

    def swap(m, way):
        return pltpu.make_async_remote_copy(
            src_ref=part.at[m, way],
            dst_ref=part_got.at[m, way],
            send_sem=sy.at[m, way],
            recv_sem=ry.at[m, way],
            device_id=peer_y,
            device_id_type=MESH,
        )

    def close_rows(m, way):
        @pl.loop(0, model_width // step)
        def _(j):
            at = pl.ds(pl.multiple_of(j * step, step), step)
            if way == 0:
                total = dot(act[of(m), :], w_out[:, at])
            else:
                total = dot_nt(gu[of(m), :], w_in[at, :])
            own[m, way, :, at] = total[:mine]
            for e in range(experts):
                start = mine + e * padded
                part[m, way, e, :, at] = total[start : start + padded].astype(bf16)

        swap(m, way).start()

    def to_source(m, way, k):
        peer = lax.rem(owner + k, experts)
        return pltpu.make_async_remote_copy(
            src_ref=part.at[m, way, peer],
            dst_ref=backs[way].at[m, owner],
            send_sem=sz.at[m, way, k],
            recv_sem=rz.at[m, way, k],
            device_id={"expert": peer},
            device_id_type=MESH,
        )

    def to_self(m, way):
        return pltpu.make_async_copy(
            part.at[m, way, owner], backs[way].at[m, owner], lz.at[m, way]
        )

    def give_back(m, way):
        swap(m, way).wait()

        @pl.loop(0, experts)
        def _(e):
            at = pl.ds(pl.multiple_of(e * padded, padded), padded)
            total = own[m, way, at, :] + part_got[m, way, e].astype(f32)
            part[m, way, e] = total.astype(bf16)

        to_self(m, way).start()

        @pl.loop(1, experts)
        def _(k):
            to_source(m, way, k).start()

    def end_back(m, way):
        to_self(m, way).wait()

        @pl.loop(1, experts)
        def _(k):
            to_source(m, way, k).wait()

    chunks = out_part.shape[0]

    def out_rows(side, j):
        start = side * (half // 2) + j * step
        return dot_tn(act[:, pl.ds(pl.multiple_of(start, step), step)], gz_buf[...])

    def to_x(j):
        return pltpu.make_async_remote_copy(
            src_ref=out_part.at[j],
            dst_ref=out_got.at[j],
            send_sem=sx.at[j],
            recv_sem=rx.at[j],
            device_id=peer_x,
            device_id_type=MESH,
        )

    def put_out(j, slot):
        return pltpu.make_async_copy(out_stage.at[slot], grad_out.at[j], st.at[slot])

    def send_out_rows():
        @pl.loop(0, chunks)
        def _(j):
            out_part[j] = out_rows(1 - row_x, j).astype(bf16)
            to_x(j).start()

    def keep_out_rows():
        for j in range(chunks):
            if j > 1:
                put_out(j - 2, j % 2).wait()
            to_x(j).wait()
            out_stage[j % 2] = out_rows(row_x, j) + out_got[j].astype(f32)
            put_out(j, j % 2).start()

    quarter = in_stage.shape[0]

    def in_rows(y, x):
        start = (2 * y + x) * quarter
        return pl.ds(pl.multiple_of(start, quarter), quarter)

    def in_copies(y):
        return (
            pltpu.make_async_copy(in_part, send_in.at[y], st.at[2]),
            pltpu.make_async_copy(in_stage, keep_in.at[y], st.at[3]),
        )

    def first_rows():
        for y in range(2):
            for kind in range(2):
                if y:
                    in_copies(0)[kind].wait()
                cols = in_rows(y, 1 - row_x if kind == 0 else row_x)

                @pl.loop(0, half // (2 * step))
                def _(j):
                    at = pl.ds(pl.multiple_of(j * 2 * step, 2 * step), 2 * step)
                    value = dot_tn(x_buf[:, cols], gu[:, at])
                    if kind == 0:
                        in_part[:, at] = value.astype(bf16)
                    else:
                        in_stage[:, at] = value

                in_copies(y)[kind].start()

    for i in range(5):
        loads[i].wait()
    open_rows(0)
    close_rows(0, 0)
    close_rows(0, 1)
    for i in range(5, 7):
        loads[i].wait()
    open_rows(1)
    close_rows(1, 0)
    give_back(0, 0)
    close_rows(1, 1)
    send_out_rows()
    give_back(0, 1)
    first_rows()
    give_back(1, 0)
    give_back(1, 1)
    keep_out_rows()
    for j in range(chunks - 2, chunks):
        put_out(j, j % 2).wait()
    for copy in in_copies(1):
        copy.wait()
    for m in range(micros):
        for way in range(2):
            end_back(m, way)


def run_experts(got_h, got_g, w_in, w_out, full, chips):
    experts = 2 * chips
    micros, _, _, padded, model_width = got_h.shape
    rows = 2 * experts * padded
    half = w_in.shape[1]
    shape = jax.ShapeDtypeStruct
    hbm = pl.BlockSpec(memory_space=pl.ANY)
    slots = shape((micros, experts, padded, model_width), bf16)
    chunks = half // 2 // 256
    quarter = model_width // 4
    spots = (micros, 2, experts, padded, model_width)
    return pl.pallas_call(
        functools.partial(expert_kernel, chips, experts),
        out_shape=[
            slots,
            slots,
            shape((2, quarter, half), f32),
            shape((2, quarter, half), bf16),
            shape((chunks, 256, model_width), f32),
        ],
        in_specs=[hbm] * 5,
        out_specs=[hbm] * 5,
        scratch_shapes=[
            pltpu.VMEM((micros * rows, model_width), bf16),
            pltpu.VMEM((micros * rows, model_width), bf16),
            pltpu.VMEM((model_width, half), bf16),
            pltpu.VMEM((half, model_width), bf16),
            pltpu.VMEM((model_width, 128), bf16),
            pltpu.VMEM((micros * rows, half), bf16),
            pltpu.VMEM((micros * rows, half), bf16),
            pltpu.VMEM((micros, 2, rows // 2, model_width), f32),
            pltpu.VMEM(spots, bf16),
            pltpu.VMEM(spots, bf16),
            pltpu.VMEM((chunks, 256, model_width), bf16),
            pltpu.VMEM((chunks, 256, model_width), bf16),
            pltpu.VMEM((2, 256, model_width), f32),
            pltpu.VMEM((quarter, half), bf16),
            pltpu.VMEM((quarter, half), f32),
            DMA((7,)),
            DMA((micros, 2)),
            DMA((micros, 2)),
            DMA((micros, 2, experts)),
            DMA((micros, 2, experts)),
            DMA((micros, 2)),
            DMA((chunks,)),
            DMA((chunks,)),
            DMA((4,)),
        ],
        compiler_params=pltpu.CompilerParams(
            collective_id=3, has_side_effects=True, vmem_limit_bytes=63 * 2**20
        ),
        name="run_experts",
    )(
        got_h.reshape(micros, rows, model_width),
        got_g.reshape(micros, rows, model_width),
        w_in,
        w_out,
        full,
    )


def end_kernel(
    chips,
    experts,
    cut,
    segments,
    routes,
    gains,
    lse,
    probs,
    tokens,
    cotangent,
    qkv_hbm,
    y1_hbm,
    returned_hbm,
    back_hbm,
    attn_hbm,
    mixed_hbm,
    hidden_hbm,
    full_hbm,
    send_in,
    keep_in,
    grad_qkv,
    grad_out,
    grad_small,
    output,
    grad_x,
    grad_in,
    full,
    x_buf,
    g_buf,
    qkv,
    y1_buf,
    returned,
    back,
    attn_in,
    mixed,
    hidden,
    out_buf,
    gx_buf,
    branch,
    gqkv,
    glog_buf,
    go_buf,
    gain_rows,
    grads,
    crecv,
    xrecv,
    yrecv,
    part_z,
    zrecv,
    got_in,
    got_y,
    keep,
    load,
    load_m,
    put,
    si,
    ri,
    siy,
    riy,
    sc,
    rc,
    sx,
    rx,
    sy,
    ry,
    sz,
    rz,
):
    block, chip, core, peer_x, peer_y, peer_core, peers_z = place_of(chips)
    micros, seq_len, model_width = tokens.shape
    width = full.shape[1]
    wide = width - cut
    row_y = block // 2
    opposite = flip(core, 1)
    wide_qkv = 3 * model_width

    late = pl.ds(wide_qkv, width - wide_qkv)
    early = pl.ds(0, wide_qkv)
    once = [
        (full_hbm.at[:, late], full.at[:, late]),
        (full_hbm.at[:, early], full.at[:, early]),
        (keep_in.at[1 - row_y], keep.at[0]),
        (keep_in.at[row_y], keep.at[1]),
        (attn_hbm, attn_in),
        (mixed_hbm, mixed),
        (hidden_hbm, hidden),
    ]
    once = [pltpu.make_async_copy(src, dst, load.at[i]) for i, (src, dst) in enumerate(once)]
    pairs = (
        (returned_hbm, returned),
        (back_hbm, back),
        (cotangent, g_buf),
        (y1_hbm, y1_buf),
        (qkv_hbm, qkv),
        (tokens, x_buf),
    )

    def load_of(i, m):
        src, dst = pairs[i]
        return pltpu.make_async_copy(src.at[m], dst.at[m], load_m.at[i, m])

    once[0].start()
    for i in range(len(pairs)):
        load_of(i, 0).start()
    once[1].start()
    for i in range(len(pairs)):
        load_of(i, 1).start()
    for copy in once[2:]:
        copy.start()

    greet([peer_x, peer_y, peer_core] + peers_z[1:])

    def in_x(j):
        return pltpu.make_async_remote_copy(
            src_ref=send_in.at[1 - row_y if j == 0 else row_y],
            dst_ref=got_in.at[j],
            send_sem=si.at[j],
            recv_sem=ri.at[j],
            device_id=peer_x,
            device_id_type=MESH,
        )

    in_y = pltpu.make_async_remote_copy(
        src_ref=got_in.at[0],
        dst_ref=got_y,
        send_sem=siy,
        recv_sem=riy,
        device_id=peer_y,
        device_id_type=MESH,
    )
    in_x(0).start()
    in_x(1).start()
    strip = 32

    def pass_in_y():
        once[2].wait()
        in_x(0).wait()

        @pl.loop(0, keep.shape[1] // strip)
        def _(j):
            at = pl.ds(pl.multiple_of(j * strip, strip), strip)
            got_in[0, at, :] = (keep[0, at, :] + got_in[0, at, :].astype(f32)).astype(bf16)

        in_y.start()

    def put_in(slot, side):
        half = keep.shape[2]
        cols = pl.ds(pl.multiple_of(side * half, half), half)
        copy = pltpu.make_async_copy(keep.at[slot], grad_in.at[:, cols], put.at[2, slot])
        copy.start()
        return copy

    def end_in():
        once[3].wait()
        in_x(1).wait()

        @pl.loop(0, keep.shape[1] // strip)
        def _(j):
            at = pl.ds(pl.multiple_of(j * strip, strip), strip)
            keep[1, at, :] = keep[1, at, :] + got_in[1, at, :].astype(f32)

        stored = [put_in(1, row_y)]
        in_y.wait()

        @pl.loop(0, keep.shape[1] // strip)
        def _(j):
            at = pl.ds(pl.multiple_of(j * strip, strip), strip)
            keep[0, at, :] = got_y[at, :].astype(f32)

        return stored + [put_in(0, 1 - row_y)]

    def put_out(m):
        return pltpu.make_async_copy(out_buf.at[m], output.at[m], put.at[0, m])

    def put_x(m):
        return pltpu.make_async_copy(gx_buf.at[m], grad_x.at[m], put.at[1, m])

    gain_rows[...] = jnp.zeros(gain_rows.shape, f32)
    scale = 1.0 / math.sqrt(model_width // HEADS)
    low_half = lanes_of((seq_len, 128)) < 64
    once[0].wait()

    @pl.loop(0, micros)
    def _(m):
        here = pl.ds(pl.multiple_of(m * seq_len, seq_len), seq_len)
        for i in range(4):
            load_of(i, m).wait()
        g = g_buf[m].astype(f32)
        route = column(routes[m])
        chosen = choose_slots(route, returned.shape[1], experts)
        moe = dot(chosen, returned[m])
        prob = probs[m]
        one_hot = one_hot_of(route)
        gate = jnp.sum(prob * one_hot, axis=1, keepdims=True)
        y1 = y1_buf[m]
        out_buf[m] = (y1 + gate * moe).astype(bf16)
        put_out(m).start()
        choice = one_hot * jnp.sum(g * moe, axis=1, keepdims=True)
        glog = (prob * (choice - jnp.sum(prob * choice, axis=1, keepdims=True))).astype(bf16)
        glog_buf[here, :] = glog
        grad_h = dot(chosen, back[m]) + dot_nt(glog, full[:, pl.ds(4 * model_width, 128)])
        n2, inv2 = normalize(y1)
        gain_rows[experts + 1 : experts + 2, :] += jnp.sum(grad_h * n2, axis=0, keepdims=True)
        gy1 = g + norm_back(grad_h * gains[1:2, :], n2, inv2)
        gx_buf[m] = gy1
        branch[here, :] = gy1.astype(bf16)
        go_buf[...] = dot_nt(branch[here, :], full[:, pl.ds(wide_qkv, model_width)]).astype(bf16)
        load_of(4, m).wait()
        load_of(5, m).wait()

        @pl.when(m == 1)
        def _():
            pass_in_y()

        allowed = allowed_pairs(segments[m])

        @pl.loop(0, model_width // 128)
        def _(pair):
            at = pl.multiple_of(pair * 128, 128)
            query = qkv[m, :, pl.ds(at, 128)]
            key = qkv[m, :, pl.ds(model_width + at, 128)]
            value = qkv[m, :, pl.ds(2 * model_width + at, 128)]
            grad_o = go_buf[:, pl.ds(at, 128)]
            parts = []
            for side in range(2):
                mine = low_half if side == 0 else jnp.logical_not(low_half)
                scores = dot_nt(jnp.where(mine, query, 0.0).astype(bf16), key) * scale
                head = lanes_of(lse.shape[1:]) == 2 * pair + side
                top = jnp.sum(jnp.where(head, lse[m], 0.0), axis=1, keepdims=True)
                p = jnp.exp(jnp.where(allowed, scores, masked_value) - top)
                gp = dot_nt(jnp.where(mine, grad_o, 0.0).astype(bf16), value)
                gs = (p * (gp - jnp.sum(p * gp, axis=1, keepdims=True))).astype(bf16)
                parts.append(
                    (dot(gs, key) * scale, dot_tn(gs, query) * scale, dot_tn(p.astype(bf16), grad_o))
                )
            for i in range(3):
                both = jnp.where(low_half, parts[0][i], parts[1][i]).astype(bf16)
                gqkv[here, pl.ds(i * model_width + at, 128)] = both

        @pl.when(m == 0)
        def _():
            once[1].wait()

        ga = dot_nt(gqkv[here, :], full[:, pl.ds(0, wide_qkv)])
        n1, inv1 = normalize(x_buf[m].astype(f32))
        gain_rows[experts : experts + 1, :] += jnp.sum(ga * n1, axis=0, keepdims=True)
        gx_buf[m] = gx_buf[m] + norm_back(ga * gains[0:1, :], n1, inv1)
        put_x(m).start()

    for copy in once[4:]:
        copy.wait()
    rows = grads.shape[3]
    span = model_width // 4

    def to_core(b):
        return pltpu.make_async_remote_copy(
            src_ref=grads.at[b, :, opposite],
            dst_ref=crecv.at[b],
            send_sem=sc.at[b],
            recv_sem=rc.at[b],
            device_id=peer_core,
            device_id_type=MESH,
        )

    @pl.loop(0, 4)
    def _(b):
        cols = pl.ds(pl.multiple_of(b * span, span), span)

        def store(start, value):
            value = value.reshape(chips, 2, rows, value.shape[1]).astype(bf16)
            grads[b, :, :, :, pl.ds(start, value.shape[3])] = value

        @pl.loop(0, wide_qkv // 512)
        def _(j):
            start = pl.multiple_of(j * 512, 512)
            store(start, dot_tn(attn_in[:, cols], gqkv[:, pl.ds(start, 512)]))

        store(wide_qkv, dot_tn(mixed[:, cols], branch[...]))
        small = dot_tn(hidden[:, cols], glog_buf[...]) + jnp.transpose(gain_rows[:, cols])
        store(4 * model_width, small)
        to_core(b).start()

    left, right = pl.ds(0, cut), pl.ds(cut, wide)
    order = list(range(chips - 1, -1, -1))
    along_x, along_y, along_z = {}, {}, {}

    def spot(k, origin, cols):
        return (flip(block, origin), flip(chip, k), core, slice(None), cols)

    def begin(k):
        step = flip(chip, k)
        for origin in (3, 1, 2, 0):
            b = flip(block, origin)
            at = (b, step, core)
            grads[at] = (grads[at].astype(f32) + crecv[b, step].astype(f32)).astype(bf16)
            if origin == 3:
                along_x[k, 0] = send(
                    grads.at[spot(k, 3, left)], xrecv.at[k, 0, :, left], sx.at[k, 0], rx.at[k, 0], peer_x
                )
                along_y[k, 0] = send(
                    grads.at[spot(k, 3, right)], yrecv.at[k, 0, :, pl.ds(0, wide)], sy.at[k, 0], ry.at[k, 0], peer_y
                )
            if origin == 1:
                along_x[k, 1] = send(
                    grads.at[spot(k, 1, left)], xrecv.at[k, 1, :, left], sx.at[k, 1], rx.at[k, 1], peer_x
                )
            if origin == 2:
                along_y[k, 1] = send(
                    grads.at[spot(k, 2, right)], yrecv.at[k, 1, :, pl.ds(0, wide)], sy.at[k, 1], ry.at[k, 1], peer_y
                )

    def relay(k):
        along_x[k, 0].wait_recv()
        at = spot(k, 2, left)
        grads[at] = (grads[at].astype(f32) + xrecv[k, 0, :, left].astype(f32)).astype(bf16)
        along_y[k, 2] = send(grads.at[at], yrecv.at[k, 2, :, left], sy.at[k, 2], ry.at[k, 2], peer_y)
        along_y[k, 0].wait_recv()
        at = spot(k, 1, right)
        grads[at] = (grads[at].astype(f32) + yrecv[k, 0, :, pl.ds(0, wide)].astype(f32)).astype(bf16)
        along_x[k, 2] = send(
            grads.at[at], xrecv.at[k, 2, :, pl.ds(0, wide)], sx.at[k, 2], rx.at[k, 2], peer_x
        )

    def finish(k):
        for turn in (1, 2):
            along_x[k, turn].wait_recv()
            along_y[k, turn].wait_recv()
        lhs = (
            grads[spot(k, 0, left)].astype(f32)
            + xrecv[k, 1, :, left].astype(f32)
            + yrecv[k, 2, :, left].astype(f32)
        )
        rhs = (
            grads[spot(k, 0, right)].astype(f32)
            + yrecv[k, 1, :, pl.ds(0, wide)].astype(f32)
            + xrecv[k, 2, :, pl.ds(0, wide)].astype(f32)
        )
        if k:
            part_z[k, :, left] = lhs.astype(bf16)
            part_z[k, :, right] = rhs.astype(bf16)
            along_z[k] = send(part_z.at[k], zrecv.at[k], sz.at[k], rz.at[k], peers_z[k])
        else:
            for j in range(1, chips):
                along_z[j].wait_recv()
                lhs = lhs + zrecv[j, :, left].astype(f32)
                rhs = rhs + zrecv[j, :, right].astype(f32)
            start = 0
            for out in (grad_qkv, grad_out, grad_small):
                w = out.shape[1]
                for lo, hi, value in ((0, cut, lhs), (cut, width, rhs)):
                    a, b = max(start, lo), min(start + w, hi)
                    if a < b:
                        out[:, a - start : b - start] = value[:, a - lo : b - lo]
                start += w

    @pl.loop(0, 4)
    def _(b):
        to_core(b).wait()

    stored = None
    for i in range(chips + 2):
        if i < chips:
            begin(order[i])
        if 0 <= i - 1 < chips:
            relay(order[i - 1])
        if i == chips:
            stored = end_in()
        if i - 2 >= 0:
            finish(order[i - 2])
    for k in order:
        for turn in range(3):
            along_x[k, turn].wait_send()
            along_y[k, turn].wait_send()
        if k:
            along_z[k].wait_send()
    for copy in stored:
        copy.wait()
    for m in range(micros):
        put_out(m).wait()
        put_x(m).wait()


def end_layer(small_inputs, big_inputs, chips):
    tokens, keep_in, full = big_inputs[0], big_inputs[-1], big_inputs[9]
    experts = 2 * chips
    micros, seq_len, model_width = tokens.shape
    spots = big_inputs[4].shape[1]
    width = full.shape[1]
    rows = model_width // (8 * chips)
    cut = (width // 128 + 1) // 2 * 128
    quarter, half = keep_in.shape[1:]
    every = micros * seq_len
    shape = jax.ShapeDtypeStruct
    vmem, hbm = pl.BlockSpec(memory_space=pltpu.VMEM), pl.BlockSpec(memory_space=pl.ANY)
    tall = (micros, seq_len, model_width)
    return pl.pallas_call(
        functools.partial(end_kernel, chips, experts, cut),
        out_shape=[
            shape((rows, 3 * model_width), f32),
            shape((rows, model_width), f32),
            shape((rows, 128), f32),
            shape(tall, bf16),
            shape(tall, f32),
            shape((quarter, 2 * half), f32),
        ],
        in_specs=[vmem] * len(small_inputs) + [hbm] * len(big_inputs),
        out_specs=[vmem] * 3 + [hbm] * 3,
        scratch_shapes=[
            pltpu.VMEM((model_width, width), bf16),
            pltpu.VMEM(tall, bf16),
            pltpu.VMEM(tall, bf16),
            pltpu.VMEM((micros, seq_len, 3 * model_width), bf16),
            pltpu.VMEM(tall, f32),
            pltpu.VMEM((micros, spots, model_width), bf16),
            pltpu.VMEM((micros, spots, model_width), bf16),
            pltpu.VMEM((every, model_width), bf16),
            pltpu.VMEM((every, model_width), bf16),
            pltpu.VMEM((every, model_width), bf16),
            pltpu.VMEM(tall, bf16),
            pltpu.VMEM(tall, f32),
            pltpu.VMEM((every, model_width), bf16),
            pltpu.VMEM((every, 3 * model_width), bf16),
            pltpu.VMEM((every, 128), bf16),
            pltpu.VMEM((seq_len, model_width), bf16),
            pltpu.VMEM((128, model_width), f32),
            pltpu.VMEM((4, chips, 2, rows, width), bf16),
            pltpu.VMEM((4, chips, rows, width), bf16),
            pltpu.VMEM((chips, 3, rows, cut), bf16),
            pltpu.VMEM((chips, 3, rows, cut), bf16),
            pltpu.VMEM((chips, rows, width), bf16),
            pltpu.VMEM((chips, rows, width), bf16),
            pltpu.VMEM((2, quarter, half), bf16),
            pltpu.VMEM((quarter, half), bf16),
            pltpu.VMEM((2, quarter, half), f32),
            DMA((7,)),
            DMA((6, micros)),
            DMA((3, micros)),
            DMA((2,)),
            DMA((2,)),
            DMA(()),
            DMA(()),
            DMA((4,)),
            DMA((4,)),
            DMA((chips, 3)),
            DMA((chips, 3)),
            DMA((chips, 3)),
            DMA((chips, 3)),
            DMA((chips,)),
            DMA((chips,)),
        ],
        compiler_params=pltpu.CompilerParams(
            collective_id=2, has_side_effects=True, vmem_limit_bytes=63 * 2**20
        ),
        name="end_layer",
    )(*small_inputs, *big_inputs)


def on_device(
    tokens,
    segment_ids,
    routes,
    cotangent,
    w_qkv,
    w_attn_out,
    w_router,
    gain_attn,
    gain_moe,
    w_expert_in,
    w_expert_out,
):
    micro_count, _, seq_len, model_width = tokens.shape
    experts = w_router.shape[1]
    chips = model_width // w_qkv.shape[0] // 8

    spare = jnp.zeros((w_qkv.shape[0], 128 - 2 - experts), bf16)
    small = jnp.concatenate([w_router, gain_attn[:, None], gain_moe[:, None], spare], axis=1)
    tokens, cotangent, segment_ids = tokens[:, 0], cotangent[:, 0], segment_ids
    routes = routes.reshape(micro_count, 1, seq_len)
    attn_in, qkv, lse, mixed, residual, hidden, probs, gains, gathered, w_in, w_out, got_g, got_h = (
        begin_layer(
            tokens,
            segment_ids,
            routes,
            cotangent,
            (w_qkv, w_attn_out, small),
            w_expert_in[0],
            w_expert_out[0],
            chips,
        )
    )
    returned, grad_back, keep_in, send_in, grad_out = run_experts(
        got_h,
        got_g,
        w_in.reshape(model_width, -1),
        w_out.reshape(-1, model_width),
        gathered,
        chips,
    )
    flat = (micro_count, -1, model_width)
    grad_qkv, grad_attn_out, small_sum, output, grad_tokens, grad_in = end_layer(
        (segment_ids, routes, gains, lse, probs),
        (
            tokens,
            cotangent,
            qkv,
            residual,
            returned.reshape(flat),
            grad_back.reshape(flat),
            attn_in.reshape(-1, model_width),
            mixed.reshape(-1, model_width),
            hidden.reshape(-1, model_width),
            gathered,
            send_in,
            keep_in,
        ),
        chips,
    )
    return (
        output[:, None],
        grad_tokens[:, None],
        grad_qkv,
        grad_attn_out,
        small_sum[:, :experts],
        small_sum[:, experts],
        small_sum[:, experts + 1],
        grad_in[None],
        grad_out.reshape(1, -1, model_width),
    )


def solution(mesh):
    rows = P(("dp", "expert"))
    seqs = P(None, ("dp", "expert"))
    owned = P("expert", "dp", None)
    return jax.shard_map(
        on_device,
        mesh=mesh,
        in_specs=(seqs, seqs, seqs, seqs, rows, rows, rows, rows, rows, owned, owned),
        out_specs=(seqs, seqs, rows, rows, rows, rows, rows, owned, owned),
        check_vma=False,
    )
```

profile of v0, /device:TPU:0, one launch (start us, length us, event | category | flops | bytes accessed | tf_op | source)
XLA Modules:
  0.0 353.7 jit_solution(6635770325138626239)
XLA Ops:
  0.7 0.1 pad.3.clone
  0.7 0.8 copy.26
  1.5 0.8 copy.27
  2.2 0.8 copy.28
  3.0 0.7 maximum_maximum_fusion.shard_small
  3.7 144.1 %begin_layer.1 = (bf16[2,256,1024]{2,1,0:T(8,128)(2,1)}, bf16[2,256,3072]{2,1,0:T(8,128)(2,1)}, f32[2,256,128]{2,1,0:T(8,128)}, bf16[2,256,1024]{2,1,0:T(8,128)(...) custom-call(bf16[2,256,1024]{2,1,0:T(8,128)(2,1)} %bitcast.27, ...), custom_call_target="tpu_custom_call" | custom-call | tf_op jit(solution)/shard_map/begin_layer/pallas_call | solution.py:430
  147.8 87.4 %run_experts.1 = (bf16[2,8,40,1024]{3,2,1,0:T(8,128)(2,1)}, bf16[2,8,40,1024]{3,2,1,0:T(8,128)(2,1)}, f32[2,256,2048]{2,1,0:T(8,128)}, bf16[2,256,2048]{2,1,0:T(8,128)(2,1)}, f32[4,256,1024]{2,1,0:T(8,128)}) custom-call(bf16[2,640,1024]{2,1,0:T(8,128)(2,1)} %bitcast.34, bf16[2,640,1024]{2,1,0:T(8,128)(2,1)} %bitcast.33, bf16[1024,2048]{1,0:T(8,128)(2,1)} %bitcast.31, ...), custom_call_target="tpu_custom_call" | custom-call | tf_op jit(solution)/shard_map/run_experts/pallas_call | solution.py:736
  235.2 104.3 %end_layer.1 = (f32[32,3072]{1,0:T(8,128)}, f32[32,1024]{1,0:T(8,128)}, f32[32,128]{1,0:T(8,128)}, bf16[2,256,1024]{2,1,0:T(8,128)(2,1)}, f32[2,256,1024]{2,1,0:T(8,128)}, /*index=5*/f32[256,4096]{1,0:T(8,128)}) custom-call(s32[2,1,256]{2,1,0:T(1,128)} %segments.3, s32[2,1,256]{2,1,0:T(1,128)} %bitcast.46, f32[2,1024]{1,0:T(2,128)} %get-tuple-element.33.gains, ...), custom_call_target="tpu_custom_call" | custom-call | tf_op jit(solution)/shard_map/end_layer/pallas_call | solution.py:1182
  339.5 0.0 copy-start.2
  339.5 1.6 slice_reduce_fusion
  341.1 1.4 copy.31
  342.4 0.0 copy-start.3
  342.4 2.3 copy.38
  344.8 0.0 copy-done.2
  344.8 0.0 copy-start.4
  344.8 1.3 copy.39
  346.1 0.0 copy-done.3
  346.1 0.7 copy.40
  346.8 0.0 copy-done.4
  346.8 0.7 copy.41
  347.5 0.5 copy-done.1
  348.0 2.1 copy.42
  350.1 1.6 copy-done
  351.7 2.0 copy.43
  (3 shorter events, 0.0 us)
Async XLA Ops:
  339.5 5.3 %copy-start.2 = (f32[2,256,1024]{2,1,0:T(8,128)S(1)}, f32[2,256,1024]{2,1,0:T(8,128)}, u32[]{:S(2)}) copy-start(f32[2,256,1024]{2,1,0:T(8,128)} %get-tuple-element.51) | copy-start | bytes 6291460
  342.4 3.6 %copy-start.3 = (f32[32,3072]{1,0:T(8,128)S(1)}, f32[32,3072]{1,0:T(8,128)}, u32[]{:S(2)}) copy-start(f32[32,3072]{1,0:T(8,128)} %get-tuple-element.88) | copy-start | bytes 1179652
  344.8 2.1 copy-start.4
  344.8 3.2 copy-start.1
  348.0 3.7 %copy-start = (f32[4,256,1024]{2,1,0:T(8,128)S(1)}, f32[4,256,1024]{2,1,0:T(8,128)}, u32[]{:S(2)}) copy-start(f32[4,256,1024]{2,1,0:T(8,128)} %get-tuple-element.56) | copy-start | bytes 12582916
where the time goes:
time: 354 us
  Pallas kernels  336 us (95%)
  local copies, waits for them, and re-layouts  16.5 us (5%)
    pallas_call x1, Pallas kernels, begin_layer(): pl.pallas_call(functools.partial(begin_kernel, chips, experts), out_shape...  144 us
    pallas_call x1, Pallas kernels, end_layer(): pl.pallas_call(functools.partial(end_kernel, chips, experts, cut), out_sh...  104 us
    pallas_call x1, Pallas kernels, run_experts(): pl.pallas_call(functools.partial(expert_kernel, chips, experts), out_shap...  87.4 us
    unnamed x18, local copies, waits for them, and re-layouts  13.4 us

commit v1 on v0

--- a/solution.py
+++ b/solution.py
@@ -238,6 +238,20 @@
             send(w_out.at[at], full_out.at[row_x, at], sw.at[3 + j], rw.at[3 + j], peer_x)
         )
 
+    from_y = []
+
+    def send_strip():
+        j = len(from_y)
+        size = w_in.shape[0] // pieces
+        at = pl.ds(j * size, size)
+        from_y.append(
+            send(
+                w_in.at[at, pl.ds((1 - row_y) * half, half)],
+                full_in.at[block, at],
+                sw.at[3 + pieces + j], rw.at[3 + pieces + j], peer_y,
+            )
+        )
+
     spread(0)
 
     def put_slots(slots, m, values):
@@ -258,14 +272,14 @@
         turn_corner(k)
         if k < pieces // 2:
             send_piece()
+            send_strip()
 
     local_in = pltpu.make_async_copy(w_in.at[:, pl.ds(row_y * half, half)], hold_in, lw.at[0])
     local_out = pltpu.make_async_copy(w_out, hold_out, lw.at[1])
     local_in.start()
     local_out.start()
-    from_y = send(
-        w_in.at[:, pl.ds((1 - row_y) * half, half)], full_in.at[block], sw.at[0], rw.at[0], peer_y
-    )
+    while len(from_y) < pieces:
+        send_strip()
     from_x = send(
         w_in.at[:, pl.ds(row_y * half, half)], full_in.at[block], sw.at[1], rw.at[1], peer_x
     )
@@ -346,7 +360,7 @@
 
     scale = 1.0 / math.sqrt(model_width // HEADS)
     low_half = lanes_of((seq_len, 128)) < 64
-    diagonal = None
+    relay_slots(0, slots_g, got_g, 0)
     for m in range(micros):
         x = tokens[m].astype(f32)
         attn_in[m] = (normalize(x)[0] * gains[0:1, :]).astype(bf16)
@@ -389,13 +403,14 @@
         logits = jnp.where(real, logits, masked_value)
         weight = jnp.where(real, jnp.exp(logits - jnp.max(logits, axis=1, keepdims=True)), 0.0)
         probs[m] = weight / jnp.sum(weight, axis=1, keepdims=True)
-        if m == 0:
-            from_y.wait_recv()
-            piece = full_in.at[flip(block, 2)]
-            diagonal = send(piece, piece, sw.at[2], rw.at[2], peer_x)
-        relay_slots(0, slots_g, got_g, m)
+        if m + 1 < micros:
+            relay_slots(0, slots_g, got_g, m + 1)
         if m:
             relay_slots(1, slots_h, got_h, m - 1)
+    for copy in from_y:
+        copy.wait_recv()
+    piece = full_in.at[flip(block, 2)]
+    diagonal = send(piece, piece, sw.at[2], rw.at[2], peer_x)
     relay_slots(1, slots_h, got_h, micros - 1)
 
     for m in range(micros):
@@ -404,7 +419,8 @@
     keep.wait()
     store_in.wait()
     store_out.wait()
-    from_y.wait_send()
+    for copy in from_y:
+        copy.wait_send()
     for copy in (from_x, diagonal, *out_x):
         copy.wait()
     for k in range(chips):
@@ -461,8 +477,8 @@
             DMA((chips, 3)),
             DMA((chips, 4)),
             DMA((chips, 4)),
-            DMA((3 + pieces,)),
-            DMA((3 + pieces,)),
+            DMA((3 + 2 * pieces,)),
+            DMA((3 + 2 * pieces,)),
             DMA((2,)),
             DMA((2, micros, experts)),
             DMA((2, micros, experts)),
@@ -527,10 +543,10 @@
 
     sources = [
         (got_h.at[0], x_buf.at[pl.ds(0, rows)]),
+        (w_in_hbm, w_in),
+        (w_out_hbm, w_out),
         (full.at[:, pl.ds(4 * model_width, 128)], router),
         (got_g.at[0], gz_buf.at[pl.ds(0, rows)]),
-        (w_in_hbm, w_in),
-        (w_out_hbm, w_out),
         (got_h.at[1], x_buf.at[pl.ds(rows, rows)]),
         (got_g.at[1], gz_buf.at[pl.ds(rows, rows)]),
     ]
@@ -546,7 +562,7 @@
     def of(m):
         return pl.ds(m * rows, rows)
 
-    def open_rows(m):
+    def gate_rows(m):
         logits = dot(x_buf[of(m), :], router[...])
         lanes = lanes_of(logits.shape)
         logits = jnp.where(lanes < experts, logits, masked_value)
@@ -556,82 +572,95 @@
         gate = picked / jnp.sum(weight, axis=1, keepdims=True)
         gz_buf[of(m), :] = (gate * gz_buf[of(m), :].astype(f32)).astype(bf16)
 
+    def open_rows(m, forward, backward):
         @pl.loop(0, half // step)
         def _(j):
             at = pl.ds(pl.multiple_of(j * step, step), step)
             u = dot(x_buf[of(m), :], w_in[:, at])
-            back = dot_nt(gz_buf[of(m), :], w_out[at, :])
             root = math.sqrt(2.0 / math.pi)
             square = u * u
             bend = jnp.tanh(root * (u + 0.044715 * (u * square)))
-            act[of(m), at] = (0.5 * u * (1.0 + bend)).astype(bf16)
-            slope = 0.5 * (1.0 + bend) + 0.5 * u * (1.0 - bend * bend) * (
-                root * (1.0 + (3.0 * 0.044715) * square)
-            )
-            gu[of(m), at] = (back * slope).astype(bf16)
-
-    def swap(m, way):
+            if forward:
+                act[of(m), at] = (0.5 * u * (1.0 + bend)).astype(bf16)
+            if backward:
+                back = dot_nt(gz_buf[of(m), :], w_out[at, :])
+                slope = 0.5 * (1.0 + bend) + 0.5 * u * (1.0 - bend * bend) * (
+                    root * (1.0 + (3.0 * 0.044715) * square)
+                )
+                gu[of(m), at] = (back * slope).astype(bf16)
+
+    wing = model_width // 2
+
+    def columns(side):
+        return pl.ds(pl.multiple_of(side * wing, wing), wing)
+
+    def swap(m, way, side):
         return pltpu.make_async_remote_copy(
-            src_ref=part.at[m, way],
-            dst_ref=part_got.at[m, way],
-            send_sem=sy.at[m, way],
-            recv_sem=ry.at[m, way],
+            src_ref=part.at[m, way, :, :, columns(side)],
+            dst_ref=part_got.at[m, way, :, :, columns(side)],
+            send_sem=sy.at[m, way, side],
+            recv_sem=ry.at[m, way, side],
             device_id=peer_y,
             device_id_type=MESH,
         )
 
     def close_rows(m, way):
-        @pl.loop(0, model_width // step)
-        def _(j):
-            at = pl.ds(pl.multiple_of(j * step, step), step)
-            if way == 0:
-                total = dot(act[of(m), :], w_out[:, at])
-            else:
-                total = dot_nt(gu[of(m), :], w_in[at, :])
-            own[m, way, :, at] = total[:mine]
-            for e in range(experts):
-                start = mine + e * padded
-                part[m, way, e, :, at] = total[start : start + padded].astype(bf16)
-
-        swap(m, way).start()
-
-    def to_source(m, way, k):
+        @pl.loop(0, 2)
+        def _(side):
+            @pl.loop(0, wing // step)
+            def _(j):
+                at = pl.ds(pl.multiple_of(side * wing + j * step, step), step)
+                if way == 0:
+                    total = dot(act[of(m), :], w_out[:, at])
+                else:
+                    total = dot_nt(gu[of(m), :], w_in[at, :])
+                own[m, way, :, at] = total[:mine]
+                for e in range(experts):
+                    start = mine + e * padded
+                    part[m, way, e, :, at] = total[start : start + padded].astype(bf16)
+
+            swap(m, way, side).start()
+
+    def to_source(m, way, side, k):
         peer = lax.rem(owner + k, experts)
         return pltpu.make_async_remote_copy(
-            src_ref=part.at[m, way, peer],
-            dst_ref=backs[way].at[m, owner],
-            send_sem=sz.at[m, way, k],
-            recv_sem=rz.at[m, way, k],
+            src_ref=part.at[m, way, peer, :, columns(side)],
+            dst_ref=backs[way].at[m, owner, :, columns(side)],
+            send_sem=sz.at[m, way, side, k],
+            recv_sem=rz.at[m, way, side, k],
             device_id={"expert": peer},
             device_id_type=MESH,
         )
 
-    def to_self(m, way):
+    def to_self(m, way, side):
         return pltpu.make_async_copy(
-            part.at[m, way, owner], backs[way].at[m, owner], lz.at[m, way]
+            part.at[m, way, owner, :, columns(side)],
+            backs[way].at[m, owner, :, columns(side)],
+            lz.at[m, way, side],
         )
 
-    def give_back(m, way):
-        swap(m, way).wait()
+    def give_back(m, way, side):
+        swap(m, way, side).wait()
 
         @pl.loop(0, experts)
         def _(e):
             at = pl.ds(pl.multiple_of(e * padded, padded), padded)
-            total = own[m, way, at, :] + part_got[m, way, e].astype(f32)
-            part[m, way, e] = total.astype(bf16)
-
-        to_self(m, way).start()
+            cols = columns(side)
+            total = own[m, way, at, cols] + part_got[m, way, e, :, cols].astype(f32)
+            part[m, way, e, :, cols] = total.astype(bf16)
+
+        to_self(m, way, side).start()
 
         @pl.loop(1, experts)
         def _(k):
-            to_source(m, way, k).start()
-
-    def end_back(m, way):
-        to_self(m, way).wait()
+            to_source(m, way, side, k).start()
+
+    def end_back(m, way, side):
+        to_self(m, way, side).wait()
 
         @pl.loop(1, experts)
         def _(k):
-            to_source(m, way, k).wait()
+            to_source(m, way, side, k).wait()
 
     chunks = out_part.shape[0]
 
@@ -696,22 +725,32 @@
 
                 in_copies(y)[kind].start()
 
-    for i in range(5):
+    loads[0].wait()
+    loads[1].wait()
+    open_rows(0, True, False)
+    loads[2].wait()
+    close_rows(0, 0)
+    loads[5].wait()
+    open_rows(1, True, False)
+    close_rows(1, 0)
+    give_back(0, 0, 0)
+    for i in (3, 4, 6):
         loads[i].wait()
-    open_rows(0)
-    close_rows(0, 0)
+    gate_rows(0)
+    gate_rows(1)
+    give_back(0, 0, 1)
+    send_out_rows()
+    give_back(1, 0, 0)
+    open_rows(0, False, True)
+    give_back(1, 0, 1)
     close_rows(0, 1)
-    for i in range(5, 7):
-        loads[i].wait()
-    open_rows(1)
-    close_rows(1, 0)
-    give_back(0, 0)
+    open_rows(1, False, True)
+    give_back(0, 1, 0)
     close_rows(1, 1)
-    send_out_rows()
-    give_back(0, 1)
+    give_back(0, 1, 1)
     first_rows()
-    give_back(1, 0)
-    give_back(1, 1)
+    give_back(1, 1, 0)
+    give_back(1, 1, 1)
     keep_out_rows()
     for j in range(chunks - 2, chunks):
         put_out(j, j % 2).wait()
@@ -719,7 +758,8 @@
         copy.wait()
     for m in range(micros):
         for way in range(2):
-            end_back(m, way)
+            end_back(m, way, 0)
+            end_back(m, way, 1)
 
 
 def run_experts(got_h, got_g, w_in, w_out, full, chips):
@@ -761,11 +801,11 @@
             pltpu.VMEM((quarter, half), bf16),
             pltpu.VMEM((quarter, half), f32),
             DMA((7,)),
-            DMA((micros, 2)),
-            DMA((micros, 2)),
-            DMA((micros, 2, experts)),
-            DMA((micros, 2, experts)),
-            DMA((micros, 2)),
+            DMA((micros, 2, 2)),
+            DMA((micros, 2, 2)),
+            DMA((micros, 2, 2, experts)),
+            DMA((micros, 2, 2, experts)),
+            DMA((micros, 2, 2)),
             DMA((chunks,)),
             DMA((chunks,)),
             DMA((4,)),
@@ -994,14 +1034,14 @@
         load_of(4, m).wait()
         load_of(5, m).wait()
 
-        @pl.when(m == 1)
-        def _():
-            pass_in_y()
-
         allowed = allowed_pairs(segments[m])
 
         @pl.loop(0, model_width // 128)
         def _(pair):
+            @pl.when((m == 1) & (pair == 4))
+            def _():
+                pass_in_y()
+
             at = pl.multiple_of(pair * 128, 128)
             query = qkv[m, :, pl.ds(at, 128)]
             key = qkv[m, :, pl.ds(model_width + at, 128)]

time: 354 us -> 337 us (0.952)
  Pallas kernels: 336 us -> 319 us
    pallas_call x1, Pallas kernels: 104 us -> 96.7 us  [end_layer(): pl.pallas_call(functools.partial(end_kernel, chips, experts, cut), out_sh...]
    pallas_call x1, Pallas kernels: 144 us -> 139 us  [begin_layer(): pl.pallas_call(functools.partial(begin_kernel, chips, experts), out_shape...]
    pallas_call x1, Pallas kernels: 87.4 us -> 83.1 us  [run_experts(): pl.pallas_call(functools.partial(expert_kernel, chips, experts), out_shap...]
where the time goes in v1:
time: 337 us
  Pallas kernels  319 us (95%)
  local copies, waits for them, and re-layouts  16.5 us (5%)
    pallas_call x1, Pallas kernels, begin_layer(): pl.pallas_call(functools.partial(begin_kernel, chips, experts), out_shape...  139 us
    pallas_call x1, Pallas kernels, end_layer(): pl.pallas_call(functools.partial(end_kernel, chips, experts, cut), out_sh...  96.7 us
    pallas_call x1, Pallas kernels, run_experts(): pl.pallas_call(functools.partial(expert_kernel, chips, experts), out_shap...  83.1 us
    unnamed x18, local copies, waits for them, and re-layouts  13.4 us

profile of v1, /device:TPU:0, one launch (start us, length us, event | category | flops | bytes accessed | tf_op | source)
XLA Modules:
  0.0 337.1 jit_solution(9001613498508432661)
XLA Ops:
  0.7 0.1 pad.3.clone
  0.7 0.8 copy.26
  1.5 0.8 copy.27
  2.2 0.8 copy.28
  3.0 0.7 maximum_maximum_fusion.shard_small
  3.7 139.3 %begin_layer.1 = (bf16[2,256,1024]{2,1,0:T(8,128)(2,1)}, bf16[2,256,3072]{2,1,0:T(8,128)(2,1)}, f32[2,256,128]{2,1,0:T(8,128)}, bf16[2,256,1024]{2,1,0:T(8,128)(...) custom-call(bf16[2,256,1024]{2,1,0:T(8,128)(2,1)} %bitcast.27, ...), custom_call_target="tpu_custom_call" | custom-call | tf_op jit(solution)/shard_map/begin_layer/pallas_call | solution.py:446
  143.0 83.1 %run_experts.1 = (bf16[2,8,40,1024]{3,2,1,0:T(8,128)(2,1)}, bf16[2,8,40,1024]{3,2,1,0:T(8,128)(2,1)}, f32[2,256,2048]{2,1,0:T(8,128)}, bf16[2,256,2048]{2,1,0:T(8,128)(2,1)}, f32[4,256,1024]{2,1,0:T(8,128)}) custom-call(bf16[2,640,1024]{2,1,0:T(8,128)(2,1)} %bitcast.34, bf16[2,640,1024]{2,1,0:T(8,128)(2,1)} %bitcast.33, bf16[1024,2048]{1,0:T(8,128)(2,1)} %bitcast.31, ...), custom_call_target="tpu_custom_call" | custom-call | tf_op jit(solution)/shard_map/run_experts/pallas_call | solution.py:776
  226.2 96.7 %end_layer.1 = (f32[32,3072]{1,0:T(8,128)}, f32[32,1024]{1,0:T(8,128)}, f32[32,128]{1,0:T(8,128)}, bf16[2,256,1024]{2,1,0:T(8,128)(2,1)}, f32[2,256,1024]{2,1,0:T(8,128)}, /*index=5*/f32[256,4096]{1,0:T(8,128)}) custom-call(s32[2,1,256]{2,1,0:T(1,128)} %segments.3, s32[2,1,256]{2,1,0:T(1,128)} %bitcast.46, f32[2,1024]{1,0:T(2,128)} %get-tuple-element.33.gains, ...), custom_call_target="tpu_custom_call" | custom-call | tf_op jit(solution)/shard_map/end_layer/pallas_call | solution.py:1222
  322.9 0.0 copy-start.2
  322.9 1.6 slice_reduce_fusion
  324.5 1.4 copy.31
  325.8 0.0 copy-start.3
  325.8 2.3 copy.38
  328.2 0.0 copy-done.2
  328.2 0.0 copy-start.4
  328.2 1.3 copy.39
  329.5 0.0 copy-done.3
  329.5 0.7 copy.40
  330.2 0.0 copy-done.4
  330.2 0.7 copy.41
  330.9 0.5 copy-done.1
  331.4 2.1 copy.42
  333.5 1.6 copy-done
  335.1 2.0 copy.43
  (3 shorter events, 0.0 us)
Async XLA Ops:
  322.9 5.3 %copy-start.2 = (f32[2,256,1024]{2,1,0:T(8,128)S(1)}, f32[2,256,1024]{2,1,0:T(8,128)}, u32[]{:S(2)}) copy-start(f32[2,256,1024]{2,1,0:T(8,128)} %get-tuple-element.51) | copy-start | bytes 6291460
  325.8 3.6 %copy-start.3 = (f32[32,3072]{1,0:T(8,128)S(1)}, f32[32,3072]{1,0:T(8,128)}, u32[]{:S(2)}) copy-start(f32[32,3072]{1,0:T(8,128)} %get-tuple-element.88) | copy-start | bytes 1179652
  328.2 2.1 copy-start.4
  328.2 3.2 copy-start.1
  331.4 3.7 %copy-start = (f32[4,256,1024]{2,1,0:T(8,128)S(1)}, f32[4,256,1024]{2,1,0:T(8,128)}, u32[]{:S(2)}) copy-start(f32[4,256,1024]{2,1,0:T(8,128)} %get-tuple-element.56) | copy-start | bytes 12582916

commit v2 on v1

--- a/solution.py
+++ b/solution.py
@@ -873,6 +873,7 @@
     yrecv,
     part_z,
     zrecv,
+    brecv,
     got_in,
     got_y,
     keep,
@@ -891,11 +892,12 @@
     ry,
     sz,
     rz,
+    sb,
+    rb,
 ):
     block, chip, core, peer_x, peer_y, peer_core, peers_z = place_of(chips)
     micros, seq_len, model_width = tokens.shape
     width = full.shape[1]
-    wide = width - cut
     row_y = block // 2
     opposite = flip(core, 1)
     wide_qkv = 3 * model_width
@@ -1106,25 +1108,47 @@
         store(4 * model_width, small)
         to_core(b).start()
 
-    left, right = pl.ds(0, cut), pl.ds(cut, wide)
+    inner = width - brecv.shape[3]
+    outer = pl.ds(inner, width - inner)
     order = list(range(chips - 1, -1, -1))
-    along_x, along_y, along_z = {}, {}, {}
+    along_x, along_y, along_z, along_b = {}, {}, {}, {}
+
+    def halves_of(k):
+        low, end = (inner // 256 * 128, inner) if k else (cut, width)
+        return pl.ds(0, low), pl.ds(low, end - low), pl.ds(0, end - low)
 
     def spot(k, origin, cols):
         return (flip(block, origin), flip(chip, k), core, slice(None), cols)
 
+    def add_core(k, origin, cols):
+        at = spot(k, origin, cols)
+        return grads[at].astype(f32) + crecv[at[:2] + at[3:]].astype(f32)
+
+    def begin_outer(k):
+        for origin in range(4):
+            at = spot(k, origin, outer)
+            grads[at] = add_core(k, origin, outer).astype(bf16)
+            along_b[k, origin] = send(
+                grads.at[at], brecv.at[k, origin], sb.at[k, origin], rb.at[k, origin], peers_z[k]
+            )
+
     def begin(k):
-        step = flip(chip, k)
+        left, right, short = halves_of(k)
         for origin in (3, 1, 2, 0):
-            b = flip(block, origin)
-            at = (b, step, core)
-            grads[at] = (grads[at].astype(f32) + crecv[b, step].astype(f32)).astype(bf16)
+            at = spot(k, origin, pl.ds(0, inner))
+            grads[at] = add_core(k, origin, pl.ds(0, inner)).astype(bf16)
+            if k == 0:
+                total = add_core(0, origin, outer)
+                for j in range(1, chips):
+                    along_b[j, origin].wait_recv()
+                    total = total + brecv[j, origin].astype(f32)
+                grads[spot(0, origin, outer)] = total.astype(bf16)
             if origin == 3:
                 along_x[k, 0] = send(
                     grads.at[spot(k, 3, left)], xrecv.at[k, 0, :, left], sx.at[k, 0], rx.at[k, 0], peer_x
                 )
                 along_y[k, 0] = send(
-                    grads.at[spot(k, 3, right)], yrecv.at[k, 0, :, pl.ds(0, wide)], sy.at[k, 0], ry.at[k, 0], peer_y
+                    grads.at[spot(k, 3, right)], yrecv.at[k, 0, :, short], sy.at[k, 0], ry.at[k, 0], peer_y
                 )
             if origin == 1:
                 along_x[k, 1] = send(
@@ -1132,22 +1156,24 @@
                 )
             if origin == 2:
                 along_y[k, 1] = send(
-                    grads.at[spot(k, 2, right)], yrecv.at[k, 1, :, pl.ds(0, wide)], sy.at[k, 1], ry.at[k, 1], peer_y
+                    grads.at[spot(k, 2, right)], yrecv.at[k, 1, :, short], sy.at[k, 1], ry.at[k, 1], peer_y
                 )
 
     def relay(k):
+        left, right, short = halves_of(k)
         along_x[k, 0].wait_recv()
         at = spot(k, 2, left)
         grads[at] = (grads[at].astype(f32) + xrecv[k, 0, :, left].astype(f32)).astype(bf16)
         along_y[k, 2] = send(grads.at[at], yrecv.at[k, 2, :, left], sy.at[k, 2], ry.at[k, 2], peer_y)
         along_y[k, 0].wait_recv()
         at = spot(k, 1, right)
-        grads[at] = (grads[at].astype(f32) + yrecv[k, 0, :, pl.ds(0, wide)].astype(f32)).astype(bf16)
+        grads[at] = (grads[at].astype(f32) + yrecv[k, 0, :, short].astype(f32)).astype(bf16)
         along_x[k, 2] = send(
-            grads.at[at], xrecv.at[k, 2, :, pl.ds(0, wide)], sx.at[k, 2], rx.at[k, 2], peer_x
+            grads.at[at], xrecv.at[k, 2, :, short], sx.at[k, 2], rx.at[k, 2], peer_x
         )
 
     def finish(k):
+        left, right, short = halves_of(k)
         for turn in (1, 2):
             along_x[k, turn].wait_recv()
             along_y[k, turn].wait_recv()
@@ -1158,22 +1184,26 @@
         )
         rhs = (
             grads[spot(k, 0, right)].astype(f32)
-            + yrecv[k, 1, :, pl.ds(0, wide)].astype(f32)
-            + xrecv[k, 2, :, pl.ds(0, wide)].astype(f32)
+            + yrecv[k, 1, :, short].astype(f32)
+            + xrecv[k, 2, :, short].astype(f32)
         )
         if k:
             part_z[k, :, left] = lhs.astype(bf16)
             part_z[k, :, right] = rhs.astype(bf16)
-            along_z[k] = send(part_z.at[k], zrecv.at[k], sz.at[k], rz.at[k], peers_z[k])
+            cols = pl.ds(0, inner)
+            along_z[k] = send(
+                part_z.at[k, :, cols], zrecv.at[k, :, cols], sz.at[k], rz.at[k], peers_z[k]
+            )
         else:
+            middle, rhs = rhs[:, : inner - cut], rhs[:, inner - cut :]
             for j in range(1, chips):
                 along_z[j].wait_recv()
                 lhs = lhs + zrecv[j, :, left].astype(f32)
-                rhs = rhs + zrecv[j, :, right].astype(f32)
+                middle = middle + zrecv[j, :, pl.ds(cut, inner - cut)].astype(f32)
             start = 0
             for out in (grad_qkv, grad_out, grad_small):
                 w = out.shape[1]
-                for lo, hi, value in ((0, cut, lhs), (cut, width, rhs)):
+                for lo, hi, value in ((0, cut, lhs), (cut, inner, middle), (inner, width, rhs)):
                     a, b = max(start, lo), min(start + w, hi)
                     if a < b:
                         out[:, a - start : b - start] = value[:, a - lo : b - lo]
@@ -1183,6 +1213,8 @@
     def _(b):
         to_core(b).wait()
 
+    for k in order[:-1]:
+        begin_outer(k)
     stored = None
     for i in range(chips + 2):
         if i < chips:
@@ -1199,6 +1231,8 @@
             along_y[k, turn].wait_send()
         if k:
             along_z[k].wait_send()
+            for origin in range(4):
+                along_b[k, origin].wait_send()
     for copy in stored:
         copy.wait()
     for m in range(micros):
@@ -1255,6 +1289,7 @@
             pltpu.VMEM((chips, 3, rows, cut), bf16),
             pltpu.VMEM((chips, rows, width), bf16),
             pltpu.VMEM((chips, rows, width), bf16),
+            pltpu.VMEM((chips, 4, rows, width // 512 * 128), bf16),
             pltpu.VMEM((2, quarter, half), bf16),
             pltpu.VMEM((quarter, half), bf16),
             pltpu.VMEM((2, quarter, half), f32),
@@ -1273,6 +1308,8 @@
             DMA((chips, 3)),
             DMA((chips,)),
             DMA((chips,)),
+            DMA((chips, 4)),
+            DMA((chips, 4)),
         ],
         compiler_params=pltpu.CompilerParams(
             collective_id=2, has_side_effects=True, vmem_limit_bytes=63 * 2**20

time: 337 us -> 334 us (level)
  Pallas kernels: 319 us -> 315 us
    pallas_call x1, Pallas kernels: 96.7 us -> 93 us  [end_layer(): pl.pallas_call(functools.partial(end_kernel, chips, experts, cut), out_sh...]
where the time goes in v2:
time: 334 us; the launch traced here: 333 us
  Pallas kernels  315 us (94%)
  local copies, waits for them, and re-layouts  16.5 us (5%)
    pallas_call x1, Pallas kernels, begin_layer(): pl.pallas_call(functools.partial(begin_kernel, chips, experts), out_shape...  139 us
    pallas_call x1, Pallas kernels, end_layer(): pl.pallas_call(functools.partial(end_kernel, chips, experts, cut), out_sh...  93 us
    pallas_call x1, Pallas kernels, run_experts(): pl.pallas_call(functools.partial(expert_kernel, chips, experts), out_shap...  83.1 us
    unnamed x18, local copies, waits for them, and re-layouts  13.4 us

profile of v2, /device:TPU:0, one launch (start us, length us, event | category | flops | bytes accessed | tf_op | source)
XLA Modules:
  0.0 333.3 jit_solution(3524233154817634215)
XLA Ops:
  0.7 0.1 pad.3.clone
  0.7 0.8 copy.26
  1.5 0.8 copy.27
  2.2 0.8 copy.28
  3.0 0.7 maximum_maximum_fusion.shard_small
  3.7 139.3 %begin_layer.1 = (bf16[2,256,1024]{2,1,0:T(8,128)(2,1)}, bf16[2,256,3072]{2,1,0:T(8,128)(2,1)}, f32[2,256,128]{2,1,0:T(8,128)}, bf16[2,256,1024]{2,1,0:T(8,128)(...) custom-call(bf16[2,256,1024]{2,1,0:T(8,128)(2,1)} %bitcast.27, ...), custom_call_target="tpu_custom_call" | custom-call | tf_op jit(solution)/shard_map/begin_layer/pallas_call | solution.py:446
  143.0 83.1 %run_experts.1 = (bf16[2,8,40,1024]{3,2,1,0:T(8,128)(2,1)}, bf16[2,8,40,1024]{3,2,1,0:T(8,128)(2,1)}, f32[2,256,2048]{2,1,0:T(8,128)}, bf16[2,256,2048]{2,1,0:T(8,128)(2,1)}, f32[4,256,1024]{2,1,0:T(8,128)}) custom-call(bf16[2,640,1024]{2,1,0:T(8,128)(2,1)} %bitcast.34, bf16[2,640,1024]{2,1,0:T(8,128)(2,1)} %bitcast.33, bf16[1024,2048]{1,0:T(8,128)(2,1)} %bitcast.31, ...), custom_call_target="tpu_custom_call" | custom-call | tf_op jit(solution)/shard_map/run_experts/pallas_call | solution.py:776
  226.2 93.0 %end_layer.1 = (f32[32,3072]{1,0:T(8,128)}, f32[32,1024]{1,0:T(8,128)}, f32[32,128]{1,0:T(8,128)}, bf16[2,256,1024]{2,1,0:T(8,128)(2,1)}, f32[2,256,1024]{2,1,0:T(8,128)}, /*index=5*/f32[256,4096]{1,0:T(8,128)}) custom-call(s32[2,1,256]{2,1,0:T(1,128)} %segments.3, s32[2,1,256]{2,1,0:T(1,128)} %bitcast.46, f32[2,1024]{1,0:T(2,128)} %get-tuple-element.33.gains, ...), custom_call_target="tpu_custom_call" | custom-call | tf_op jit(solution)/shard_map/end_layer/pallas_call | solution.py:1256
  319.1 0.0 copy-start.2
  319.1 1.6 slice_reduce_fusion
  320.7 1.4 copy.31
  322.1 0.0 copy-start.3
  322.1 2.3 copy.38
  324.4 0.0 copy-done.2
  324.4 0.0 copy-start.4
  324.4 1.3 copy.39
  325.7 0.0 copy-done.3
  325.7 0.7 copy.40
  326.5 0.0 copy-done.4
  326.5 0.7 copy.41
  327.1 0.5 copy-done.1
  327.6 2.1 copy.42
  329.8 1.6 copy-done
  331.3 2.0 copy.43
  (3 shorter events, 0.0 us)
Async XLA Ops:
  319.1 5.3 %copy-start.2 = (f32[2,256,1024]{2,1,0:T(8,128)S(1)}, f32[2,256,1024]{2,1,0:T(8,128)}, u32[]{:S(2)}) copy-start(f32[2,256,1024]{2,1,0:T(8,128)} %get-tuple-element.51) | copy-start | bytes 6291460
  322.1 3.6 %copy-start.3 = (f32[32,3072]{1,0:T(8,128)S(1)}, f32[32,3072]{1,0:T(8,128)}, u32[]{:S(2)}) copy-start(f32[32,3072]{1,0:T(8,128)} %get-tuple-element.88) | copy-start | bytes 1179652
  324.4 2.1 copy-start.4
  324.4 3.2 copy-start.1
  327.6 3.7 %copy-start = (f32[4,256,1024]{2,1,0:T(8,128)S(1)}, f32[4,256,1024]{2,1,0:T(8,128)}, u32[]{:S(2)}) copy-start(f32[4,256,1024]{2,1,0:T(8,128)} %get-tuple-element.56) | copy-start | bytes 12582916

commit v3 on v2

--- a/solution.py
+++ b/solution.py
@@ -153,6 +153,8 @@
     ry,
     sc,
     rc,
+    sb,
+    rb,
     sw,
     rw,
     lw,
@@ -167,9 +169,13 @@
     micros, seq_len, model_width = tokens.shape
     rows = shard_qkv.shape[0]
     width = full.shape[1]
-    cut = (width // 128 + 1) // 2 * 128
-    halves = (pl.ds(0, cut), pl.ds(cut, width - cut))
+    cut = width // 128 * 5 // 8 * 128
     every = pl.ds(0, width)
+    inner = width // 128 * 5 // 6 * 128
+    cut_in = inner // 256 * 128
+    outer = pl.ds(inner, width - inner)
+    halves_of = [(pl.ds(0, cut), pl.ds(cut, width - cut))]
+    halves_of += [(pl.ds(0, cut_in), pl.ds(cut_in, inner - cut_in))] * (chips - 1)
     half = w_in.shape[1] // 2
     row_y, row_x = block // 2, block % 2
 
@@ -193,22 +199,34 @@
     along_z = [None] + [send(mine, mine, sz.at[k], rz.at[k], peers_z[k]) for k in range(1, chips)]
     along_x = [[None] * 3 for _ in range(chips)]
     along_y = [[None] * 3 for _ in range(chips)]
-    across = [[None] * 4 for _ in range(chips)]
-
-    def to_core(k, origin):
-        piece = part(origin, k, every)
-        across[k][origin] = send(
-            piece, piece, sc.at[k, origin], rc.at[k, origin], peer_core
-        )
+    across = [[None] * 8 for _ in range(chips)]
+    along_b = [[None] * 4 for _ in range(chips)]
+
+    def to_core(k, origin, columns, tail=0):
+        piece = part(origin, k, columns)
+        at = (k, origin + 4 * tail)
+        across[k][at[1]] = send(piece, piece, sc.at[at], rc.at[at], peer_core)
+
+    def to_chips(origin):
+        piece = part(origin, 0, outer)
+        for k in range(1, chips):
+            along_b[k][origin] = send(
+                piece, piece, sb.at[k, origin], rb.at[k, origin], peers_z[k]
+            )
 
     def pass_on(k):
+        columns = pl.ds(0, inner) if k else every
         along_x[k][1].wait_recv()
-        to_core(k, 1)
+        if k == 0:
+            to_chips(1)
+        to_core(k, 1, columns)
         along_y[k][1].wait_recv()
-        to_core(k, 2)
+        to_core(k, 2, columns)
         along_x[k][2].wait_recv()
+        if k == 0:
+            to_chips(3)
         along_y[k][2].wait_recv()
-        to_core(k, 3)
+        to_core(k, 3, columns)
 
     def spread(k):
         for turn in range(2):
@@ -216,16 +234,18 @@
                 (along_x, sx, rx, peer_x, turn),
                 (along_y, sy, ry, peer_y, 1 - turn),
             ):
-                piece = part(0, k, halves[side])
+                piece = part(0, k, halves_of[k][side])
                 copies[k][turn] = send(piece, piece, s.at[k, turn], r.at[k, turn], peer)
-        to_core(k, 0)
+        to_core(k, 0, every)
 
     def turn_corner(k):
         along_x[k][0].wait_recv()
-        piece = part(1, k, halves[0])
+        piece = part(1, k, halves_of[k][0])
         along_y[k][2] = send(piece, piece, sy.at[k, 2], ry.at[k, 2], peer_y)
         along_y[k][0].wait_recv()
-        piece = part(2, k, halves[1])
+        if k == 0:
+            to_chips(2)
+        piece = part(2, k, halves_of[k][1])
         along_x[k][2] = send(piece, piece, sx.at[k, 2], rx.at[k, 2], peer_x)
 
     piece_rows = w_out.shape[0] // pieces
@@ -344,9 +364,14 @@
     for m in range(micros):
         start_slots(0, slots_g, got_g, m)
     pass_on(chips - 1)
+    for k in range(1, chips):
+        for origin in range(1, 4):
+            along_b[k][origin].wait_recv()
+            to_core(k, origin, outer, 1)
     for k in range(chips):
-        for origin in range(4):
-            across[k][origin].wait_recv()
+        for copy in across[k]:
+            if copy is not None:
+                copy.wait_recv()
     keep = pltpu.make_async_copy(full, kept_full, own_sem.at[3])
     keep.start()
     small = jnp.transpose(full[:, pl.ds(4 * model_width, 128)].astype(f32))
@@ -429,8 +454,9 @@
         for turn in range(3):
             along_x[k][turn].wait_send()
             along_y[k][turn].wait_send()
-        for origin in range(4):
-            across[k][origin].wait_send()
+        for copy in across[k] + along_b[k]:
+            if copy is not None:
+                copy.wait_send()
 
 
 def begin_layer(tokens, segments, routes, cotangent, shards, w_in, w_out, chips):
@@ -475,6 +501,8 @@
             DMA((chips, 3)),
             DMA((chips, 3)),
             DMA((chips, 3)),
+            DMA((chips, 8)),
+            DMA((chips, 8)),
             DMA((chips, 4)),
             DMA((chips, 4)),
             DMA((3 + 2 * pieces,)),

time: 334 us -> 331 us (level)
    pallas_call x1, Pallas kernels: 139 us -> 135 us  [begin_layer(): pl.pallas_call(functools.partial(begin_kernel, chips, experts), out_shape...]
where the time goes in v3:
time: 331 us
  Pallas kernels  313 us (95%)
  local copies, waits for them, and re-layouts  16.5 us (5%)
    pallas_call x1, Pallas kernels, begin_layer(): pl.pallas_call(functools.partial(begin_kernel, chips, experts), out_shape...  135 us
    pallas_call x1, Pallas kernels, end_layer(): pl.pallas_call(functools.partial(end_kernel, chips, experts, cut), out_sh...  94.3 us
    pallas_call x1, Pallas kernels, run_experts(): pl.pallas_call(functools.partial(expert_kernel, chips, experts), out_shap...  83.4 us
    unnamed x18, local copies, waits for them, and re-layouts  13.4 us

profile of v3, /device:TPU:0, one launch (start us, length us, event | category | flops | bytes accessed | tf_op | source)
XLA Modules:
  0.0 330.8 jit_solution(15772298255100571653)
XLA Ops:
  0.7 0.1 pad.3.clone
  0.7 0.8 copy.26
  1.5 0.8 copy.27
  2.2 0.8 copy.28
  3.0 0.7 maximum_maximum_fusion.shard_small
  3.7 135.2 %begin_layer.1 = (bf16[2,256,1024]{2,1,0:T(8,128)(2,1)}, bf16[2,256,3072]{2,1,0:T(8,128)(2,1)}, f32[2,256,128]{2,1,0:T(8,128)}, bf16[2,256,1024]{2,1,0:T(8,128)(...) custom-call(bf16[2,256,1024]{2,1,0:T(8,128)(2,1)} %bitcast.27, ...), custom_call_target="tpu_custom_call" | custom-call | tf_op jit(solution)/shard_map/begin_layer/pallas_call | solution.py:472
  138.9 83.4 %run_experts.1 = (bf16[2,8,40,1024]{3,2,1,0:T(8,128)(2,1)}, bf16[2,8,40,1024]{3,2,1,0:T(8,128)(2,1)}, f32[2,256,2048]{2,1,0:T(8,128)}, bf16[2,256,2048]{2,1,0:T(8,128)(2,1)}, f32[4,256,1024]{2,1,0:T(8,128)}) custom-call(bf16[2,640,1024]{2,1,0:T(8,128)(2,1)} %bitcast.34, bf16[2,640,1024]{2,1,0:T(8,128)(2,1)} %bitcast.33, bf16[1024,2048]{1,0:T(8,128)(2,1)} %bitcast.31, ...), custom_call_target="tpu_custom_call" | custom-call | tf_op jit(solution)/shard_map/run_experts/pallas_call | solution.py:804
  222.3 94.3 %end_layer.1 = (f32[32,3072]{1,0:T(8,128)}, f32[32,1024]{1,0:T(8,128)}, f32[32,128]{1,0:T(8,128)}, bf16[2,256,1024]{2,1,0:T(8,128)(2,1)}, f32[2,256,1024]{2,1,0:T(8,128)}, /*index=5*/f32[256,4096]{1,0:T(8,128)}) custom-call(s32[2,1,256]{2,1,0:T(1,128)} %segments.3, s32[2,1,256]{2,1,0:T(1,128)} %bitcast.46, f32[2,1024]{1,0:T(2,128)} %get-tuple-element.33.gains, ...), custom_call_target="tpu_custom_call" | custom-call | tf_op jit(solution)/shard_map/end_layer/pallas_call | solution.py:1284
  316.6 0.0 copy-start.2
  316.6 1.6 slice_reduce_fusion
  318.2 1.4 copy.31
  319.6 0.0 copy-start.3
  319.6 2.3 copy.38
  321.9 0.0 copy-done.2
  321.9 0.0 copy-start.4
  321.9 1.3 copy.39
  323.2 0.0 copy-done.3
  323.2 0.7 copy.40
  324.0 0.0 copy-done.4
  324.0 0.7 copy.41
  324.6 0.5 copy-done.1
  325.1 2.1 copy.42
  327.2 1.6 copy-done
  328.8 2.0 copy.43
  (3 shorter events, 0.0 us)
Async XLA Ops:
  316.6 5.3 %copy-start.2 = (f32[2,256,1024]{2,1,0:T(8,128)S(1)}, f32[2,256,1024]{2,1,0:T(8,128)}, u32[]{:S(2)}) copy-start(f32[2,256,1024]{2,1,0:T(8,128)} %get-tuple-element.51) | copy-start | bytes 6291460
  319.6 3.6 %copy-start.3 = (f32[32,3072]{1,0:T(8,128)S(1)}, f32[32,3072]{1,0:T(8,128)}, u32[]{:S(2)}) copy-start(f32[32,3072]{1,0:T(8,128)} %get-tuple-element.88) | copy-start | bytes 1179652
  321.9 2.1 copy-start.4
  321.9 3.2 copy-start.1
  325.1 3.7 %copy-start = (f32[4,256,1024]{2,1,0:T(8,128)S(1)}, f32[4,256,1024]{2,1,0:T(8,128)}, u32[]{:S(2)}) copy-start(f32[4,256,1024]{2,1,0:T(8,128)} %get-tuple-element.56) | copy-start | bytes 12582916

commit v4 on v3

--- a/solution.py
+++ b/solution.py
@@ -1068,7 +1068,7 @@
 
         @pl.loop(0, model_width // 128)
         def _(pair):
-            @pl.when((m == 1) & (pair == 4))
+            @pl.when((m == 1) & (pair == 3))
             def _():
                 pass_in_y()
 
@@ -1317,7 +1317,7 @@
             pltpu.VMEM((chips, 3, rows, cut), bf16),
             pltpu.VMEM((chips, rows, width), bf16),
             pltpu.VMEM((chips, rows, width), bf16),
-            pltpu.VMEM((chips, 4, rows, width // 512 * 128), bf16),
+            pltpu.VMEM((chips, 4, rows, width // 640 * 128), bf16),
             pltpu.VMEM((2, quarter, half), bf16),
             pltpu.VMEM((quarter, half), bf16),
             pltpu.VMEM((2, quarter, half), f32),

time: 331 us -> 331 us (level)
  no operation moved by 1% of the time
where the time goes in v4:
time: 331 us; the launch traced here: 330 us
  Pallas kernels  312 us (94%)
  local copies, waits for them, and re-layouts  16.5 us (5%)
    pallas_call x1, Pallas kernels, begin_layer(): pl.pallas_call(functools.partial(begin_kernel, chips, experts), out_shape...  135 us
    pallas_call x1, Pallas kernels, end_layer(): pl.pallas_call(functools.partial(end_kernel, chips, experts, cut), out_sh...  93.9 us
    pallas_call x1, Pallas kernels, run_experts(): pl.pallas_call(functools.partial(expert_kernel, chips, experts), out_shap...  83.4 us
    unnamed x18, local copies, waits for them, and re-layouts  13.4 us

profile of v4, /device:TPU:0, one launch (start us, length us, event | category | flops | bytes accessed | tf_op | source)
XLA Modules:
  0.0 330.4 jit_solution(14265115399789700923)
XLA Ops:
  0.7 0.1 pad.3.clone
  0.7 0.8 copy.26
  1.5 0.8 copy.27
  2.2 0.8 copy.28
  3.0 0.7 maximum_maximum_fusion.shard_small
  3.7 135.2 %begin_layer.1 = (bf16[2,256,1024]{2,1,0:T(8,128)(2,1)}, bf16[2,256,3072]{2,1,0:T(8,128)(2,1)}, f32[2,256,128]{2,1,0:T(8,128)}, bf16[2,256,1024]{2,1,0:T(8,128)(...) custom-call(bf16[2,256,1024]{2,1,0:T(8,128)(2,1)} %bitcast.27, ...), custom_call_target="tpu_custom_call" | custom-call | tf_op jit(solution)/shard_map/begin_layer/pallas_call | solution.py:472
  138.9 83.4 %run_experts.1 = (bf16[2,8,40,1024]{3,2,1,0:T(8,128)(2,1)}, bf16[2,8,40,1024]{3,2,1,0:T(8,128)(2,1)}, f32[2,256,2048]{2,1,0:T(8,128)}, bf16[2,256,2048]{2,1,0:T(8,128)(2,1)}, f32[4,256,1024]{2,1,0:T(8,128)}) custom-call(bf16[2,640,1024]{2,1,0:T(8,128)(2,1)} %bitcast.34, bf16[2,640,1024]{2,1,0:T(8,128)(2,1)} %bitcast.33, bf16[1024,2048]{1,0:T(8,128)(2,1)} %bitcast.31, ...), custom_call_target="tpu_custom_call" | custom-call | tf_op jit(solution)/shard_map/run_experts/pallas_call | solution.py:804
  222.3 93.9 %end_layer.1 = (f32[32,3072]{1,0:T(8,128)}, f32[32,1024]{1,0:T(8,128)}, f32[32,128]{1,0:T(8,128)}, bf16[2,256,1024]{2,1,0:T(8,128)(2,1)}, f32[2,256,1024]{2,1,0:T(8,128)}, /*index=5*/f32[256,4096]{1,0:T(8,128)}) custom-call(s32[2,1,256]{2,1,0:T(1,128)} %segments.3, s32[2,1,256]{2,1,0:T(1,128)} %bitcast.46, f32[2,1024]{1,0:T(2,128)} %get-tuple-element.33.gains, ...), custom_call_target="tpu_custom_call" | custom-call | tf_op jit(solution)/shard_map/end_layer/pallas_call | solution.py:1284
  316.2 0.0 copy-start.2
  316.2 1.6 slice_reduce_fusion
  317.8 1.4 copy.31
  319.2 0.0 copy-start.3
  319.2 2.3 copy.38
  321.5 0.0 copy-done.2
  321.5 0.0 copy-start.4
  321.5 1.3 copy.39
  322.8 0.0 copy-done.3
  322.8 0.7 copy.40
  323.6 0.0 copy-done.4
  323.6 0.7 copy.41
  324.2 0.5 copy-done.1
  324.7 2.1 copy.42
  326.8 1.6 copy-done
  328.4 2.0 copy.43
  (3 shorter events, 0.0 us)
Async XLA Ops:
  316.2 5.3 %copy-start.2 = (f32[2,256,1024]{2,1,0:T(8,128)S(1)}, f32[2,256,1024]{2,1,0:T(8,128)}, u32[]{:S(2)}) copy-start(f32[2,256,1024]{2,1,0:T(8,128)} %get-tuple-element.51) | copy-start | bytes 6291460
  319.2 3.6 %copy-start.3 = (f32[32,3072]{1,0:T(8,128)S(1)}, f32[32,3072]{1,0:T(8,128)}, u32[]{:S(2)}) copy-start(f32[32,3072]{1,0:T(8,128)} %get-tuple-element.88) | copy-start | bytes 1179652
  321.5 2.1 copy-start.4
  321.5 3.2 copy-start.1
  324.7 3.7 %copy-start = (f32[4,256,1024]{2,1,0:T(8,128)S(1)}, f32[4,256,1024]{2,1,0:T(8,128)}, u32[]{:S(2)}) copy-start(f32[4,256,1024]{2,1,0:T(8,128)} %get-tuple-element.56) | copy-start | bytes 12582916
